TPU v7x, 512 devices: a whole 4x8x8 slice. The times are simulated.
512 devices in a mesh: seq: 128 (over z, y, core), head: 4 (over x).
Axes of the slice: x: 4, y: 8, z: 8, core: 2. Of those that a mesh axis runs over, the one named last changes fastest.
Arguments:
- queries: bfloat16 [32768, 4096], P('seq', 'head'), may hold values from -6 to 6
- keys: bfloat16 [32768, 512], P(('seq', 'head')), may hold values from -6 to 6
- values: bfloat16 [32768, 512], P(('seq', 'head')), may hold values from -6 to 6
- d_out: bfloat16 [32768, 4096], P('seq', 'head'), may hold values from -6 to 6
- rand_blocks: int32 [512, 8], P('seq'), may hold values from 0 to 511, as said below
- glob_blocks: int32 [2], replicated, may hold values from 0 to 511
Outputs:
- attn_out: bfloat16 [32768, 4096], P('seq', 'head')
- d_queries: bfloat16 [32768, 4096], P('seq', 'head')
- d_keys: bfloat16 [32768, 512], P(('seq', 'head'))
- d_values: bfloat16 [32768, 512], P(('seq', 'head'))
Inputs may be any that keep to these rules, and one draw needn't show every extreme that they name: `rand_blocks`: block b lies on index b // 4 of seq. Among the 32 entries of the query blocks of one index of seq, at most 1 name blocks of any one index, and some index of seq reaches 1 for some owner in every draw.
All inputs are finite; a program needn't handle non-finite values.
Results may differ from a plain program's by a relative error of at most 0.012.
Values may be sent and summed in bfloat16 or wider, within the bound.
A program may use at most 64 MiB of HBM per device.

v0:
```python
import jax
import jax.numpy as jnp
from jax import lax
from jax.sharding import PartitionSpec as P

DH = 128
KVH = 4
BLOCK = 64
GLOB = 2
RAND = 8
NEG_FILL = -1e30


def padded_2(cells, sides, width):
    for axis, dim in sides:
        count = lax.axis_size(axis)
        ends = count - 1
        head = lax.slice_in_dim(cells, 0, width, axis=dim)
        tail = lax.slice_in_dim(cells, cells.shape[dim] - width, cells.shape[dim], axis=dim)
        cells = jnp.concatenate(
            [
                lax.ppermute(tail, axis, [(i, (i + 1) % count) for i in range(ends)]),
                cells,
                lax.ppermute(head, axis, [((i + 1) % count, i) for i in range(ends)]),
            ],
            axis=dim,
        )
    return cells


def broadcast(block, axis, source):
    block = jnp.where(lax.axis_index(axis) == source, block, jnp.zeros_like(block))
    return lax.psum(block, axis)


def key_rows(library, spots):
    chosen = library[spots]
    flat = chosen.reshape(chosen.shape[0] * chosen.shape[1], chosen.shape[2])
    return (flat[:, :DH], flat[:, DH:])


def masked_scores(query_block, keys_here, allowed_row):
    factor = DH ** (-0.5)
    scores = (
        jnp.einsum("thd,kd->htk", query_block, keys_here, preferred_element_type=jnp.float32)
        * factor
    )
    widened = jnp.repeat(allowed_row, keys_here.shape[0] // allowed_row.shape[0])
    return jnp.where(widened[None, None, :], scores, NEG_FILL)


def body(queries, keys, values, d_out, rand_blocks, glob_blocks):
    seq_count = lax.axis_size("seq")
    here = lax.axis_index("seq")
    short = keys.shape[0]
    stacked = jnp.concatenate(
        [keys.reshape(short, KVH, DH), values.reshape(short, KVH, DH)], axis=2
    )
    mine = lax.all_to_all(stacked, "head", split_axis=1, concat_axis=0, tiled=True)
    tok_count = mine.shape[0]
    blocks_here = tok_count // BLOCK
    flat_pairs = mine.reshape(tok_count, 2 * DH)
    own_blocks = flat_pairs.reshape(blocks_here, BLOCK, 2 * DH)
    padded = padded_2(flat_pairs, (("seq", 0),), BLOCK)
    window = padded.reshape(blocks_here + 2, BLOCK, 2 * DH)
    global_parts = []
    for number in range(GLOB):
        target = glob_blocks[number]
        piece = lax.dynamic_index_in_dim(own_blocks, target % blocks_here, 0, keepdims=False)
        global_parts.append(broadcast(piece, "seq", target // blocks_here))
    global_pairs = jnp.stack(global_parts)
    entries = rand_blocks.reshape(-1)
    entry_count = entries.shape[0]
    capacity = -(-entry_count // seq_count)
    position_count = seq_count * capacity
    owners = entries // blocks_here
    inner_index = entries % blocks_here
    order = jnp.arange(entry_count, dtype=jnp.int32)
    earlier = (owners[:, None] == owners[None, :]) & (order[:, None] > order[None, :])
    ranks = jnp.sum(earlier.astype(jnp.int32), axis=1)
    slots = owners * capacity + ranks
    placing = slots[None, :] == jnp.arange(position_count, dtype=jnp.int32)[:, None]
    wanted = jnp.sum(jnp.where(placing, inner_index[None, :], 0), axis=1).reshape(
        seq_count, capacity
    )
    incoming = lax.all_to_all(wanted, "seq", split_axis=0, concat_axis=0, tiled=True).reshape(
        position_count
    )
    served = own_blocks[incoming].reshape(seq_count, capacity, BLOCK, 2 * DH)
    fetched = lax.all_to_all(served, "seq", split_axis=0, concat_axis=0, tiled=True).reshape(
        position_count, BLOCK, 2 * DH
    )
    block_ids = jnp.arange(blocks_here, dtype=jnp.int32)
    window_ids = jnp.stack([block_ids, block_ids + 1, block_ids + 2], axis=1)
    global_ids = jnp.broadcast_to(
        blocks_here + 2 + jnp.arange(GLOB, dtype=jnp.int32), (blocks_here, GLOB)
    )
    random_ids = blocks_here + 2 + GLOB + slots.reshape(blocks_here, RAND)
    positions = jnp.concatenate([window_ids, global_ids, random_ids], axis=1)
    allowed = jnp.concatenate(
        [
            jnp.logical_not((block_ids == 0) & (here == 0))[:, None],
            jnp.ones((blocks_here, 1), jnp.bool_),
            jnp.logical_not((block_ids == blocks_here - 1) & (here == seq_count - 1))[:, None],
            jnp.ones((blocks_here, GLOB + RAND), jnp.bool_),
        ],
        axis=1,
    )
    library = jnp.concatenate([window, global_pairs, fetched], axis=0)
    heads_here = queries.shape[1] // DH
    query_blocks = queries.reshape(blocks_here, BLOCK, heads_here, DH)
    grad_blocks = d_out.reshape(blocks_here, BLOCK, heads_here, DH)

    def forward_step(inputs):
        query_block, spots, allowed_row = inputs
        keys_here, values_here = key_rows(library, spots)
        scores = masked_scores(query_block, keys_here, allowed_row)
        peak = jnp.max(scores, axis=-1, keepdims=True)
        logsum = peak + jnp.log(jnp.sum(jnp.exp(scores - peak), axis=-1, keepdims=True))
        probs16 = jnp.exp(scores - logsum).astype(jnp.bfloat16)
        result = jnp.einsum("htk,kd->thd", probs16, values_here, preferred_element_type=jnp.float32)
        return (result.astype(jnp.bfloat16), logsum)

    out_blocks, logsums = lax.map(forward_step, (query_blocks, positions, allowed))
    refetched = lax.all_to_all(served, "seq", split_axis=0, concat_axis=0, tiled=True).reshape(
        position_count, BLOCK, 2 * DH
    )
    library_back = jnp.concatenate([window, global_pairs, refetched], axis=0)

    def backward_step(inputs):
        query_block, gradient_tile, out_block, logsum, spots, allowed_row = inputs
        keys_here, values_here = key_rows(library_back, spots)
        factor = DH ** (-0.5)
        scores = masked_scores(query_block, keys_here, allowed_row)
        probs = jnp.exp(scores - logsum)
        probs16 = probs.astype(jnp.bfloat16)
        delta = jnp.sum(gradient_tile.astype(jnp.float32) * out_block.astype(jnp.float32), axis=-1)
        dprobs = jnp.einsum(
            "thd,kd->htk", gradient_tile, values_here, preferred_element_type=jnp.float32
        )
        dscores = (probs * (dprobs - jnp.transpose(delta)[:, :, None])).astype(jnp.bfloat16)
        dquery = (
            jnp.einsum("htk,kd->thd", dscores, keys_here, preferred_element_type=jnp.float32)
            * factor
        )
        dkey = (
            jnp.einsum("htk,thd->kd", dscores, query_block, preferred_element_type=jnp.float32)
            * factor
        )
        dvalue = jnp.einsum(
            "htk,thd->kd", probs16, gradient_tile, preferred_element_type=jnp.float32
        )
        terms = jnp.concatenate([dkey, dvalue], axis=1).reshape(spots.shape[0], BLOCK, 2 * DH)
        return (dquery.astype(jnp.bfloat16), terms)

    dquery_blocks, terms = lax.map(
        backward_step, (query_blocks, grad_blocks, out_blocks, logsums, positions, allowed)
    )
    attn_out = out_blocks.reshape(tok_count, heads_here * DH)
    d_queries = dquery_blocks.reshape(tok_count, heads_here * DH)
    prev_terms = terms[:, 0]
    self_terms = terms[:, 1]
    next_terms = terms[:, 2]
    zero_block = jnp.zeros((1, BLOCK, 2 * DH), jnp.float32)
    grads = (
        self_terms
        + jnp.concatenate([prev_terms[1:], zero_block], axis=0)
        + jnp.concatenate([zero_block, next_terms[:-1]], axis=0)
    )
    rims = jnp.concatenate([prev_terms[0], next_terms[-1]], axis=0).astype(jnp.bfloat16)
    arrived = padded_2(rims, (("seq", 0),), BLOCK)
    from_left = arrived[:BLOCK].astype(jnp.float32)
    from_right = arrived[3 * BLOCK :].astype(jnp.float32)
    edge_first = jnp.concatenate(
        [from_left[None], jnp.zeros((blocks_here - 1, BLOCK, 2 * DH), jnp.float32)], axis=0
    )
    edge_last = jnp.concatenate(
        [jnp.zeros((blocks_here - 1, BLOCK, 2 * DH), jnp.float32), from_right[None]], axis=0
    )
    grads = grads + edge_first + edge_last
    global_terms = jnp.sum(terms[:, 3 : 3 + GLOB], axis=0)
    global_total = lax.psum(global_terms, "seq")
    global_hits = ((glob_blocks // blocks_here)[:, None] == here) & (
        (glob_blocks % blocks_here)[:, None] == block_ids[None, :]
    )
    grads = grads + jnp.sum(
        jnp.where(global_hits[:, :, None, None], global_total[:, None], 0.0), axis=0
    )
    random_terms = terms[:, 3 + GLOB :].reshape(entry_count, BLOCK * 2 * DH).astype(jnp.bfloat16)
    outgoing = jnp.dot(
        placing.astype(jnp.bfloat16), random_terms, preferred_element_type=jnp.float32
    ).astype(jnp.bfloat16)
    returned = lax.all_to_all(
        outgoing.reshape(seq_count, capacity, BLOCK, 2 * DH),
        "seq",
        split_axis=0,
        concat_axis=0,
        tiled=True,
    )
    landing = (incoming[None, :] == block_ids[:, None]).astype(jnp.bfloat16)
    grads = grads + jnp.dot(
        landing,
        returned.reshape(position_count, BLOCK * 2 * DH),
        preferred_element_type=jnp.float32,
    ).reshape(blocks_here, BLOCK, 2 * DH)
    packed = grads.astype(jnp.bfloat16).reshape(tok_count, 1, 2 * DH)
    restored = lax.all_to_all(packed, "head", split_axis=0, concat_axis=1, tiled=True)
    d_keys = restored[:, :, :DH].reshape(short, KVH * DH)
    d_values = restored[:, :, DH:].reshape(short, KVH * DH)
    return (attn_out, d_queries, d_keys, d_values)


def solution(mesh):
    in_specs = (
        P("seq", "head"),
        P(("seq", "head"), None),
        P(("seq", "head"), None),
        P("seq", "head"),
        P("seq", None),
        P(),
    )
    out_specs = (
        P("seq", "head"),
        P("seq", "head"),
        P(("seq", "head"), None),
        P(("seq", "head"), None),
    )
    return jax.shard_map(body, mesh=mesh, in_specs=in_specs, out_specs=out_specs, check_vma=False)
```

profile of v0, /device:TPU:1, one launch (start us, length us, event | category | flops | bytes accessed | tf_op | source)
XLA Modules:
  0.0 672.8 jit_solution(9760338004758471083)
XLA Ops:
  7.2 0.8 reshape.390
  9.0 18.4 %all-to-all-start.1 = ((s32[128,1,1]{2,1,0:T(1,128)}), s32[128,1,1]{2,1,0:T(1,128)S(1)}, u32[]{:S(2)}, u32[]{:S(2)}) async-start(s32[128,1,1]{2,1,0:T(1,128)} %copy.90), calls=%async_computation.1 | async-start | bytes 131072 | tf_op jit(solution)/shard_map/all_to_all | solution.py:86
  27.4 0.9 copy_bitcast_fusion.7
  29.0 9.9 %all-to-all-done.1 = s32[128,1,1]{2,1,0:T(1,128)S(1)} async-done(((s32[128,1,1]{2,1,0:T(1,128)}), s32[128,1,1]{2,1,0:T(1,128)S(1)}, u32[]{:S(2)}, u32[]{:S(2)}) %all-to-all-start.1) | async-done | bytes 544 | tf_op jit(solution)/shard_map/all_to_all | solution.py:86
  38.9 4.0 all-to-all-start
  42.9 2.3 reduce
  45.2 2.5 all-to-all-done
  47.7 2.8 gather_fusion.2
  50.5 8.4 %all-to-all-start.2 = ((bf16[128,1,64,256]{3,2,1,0:T(8,128)(2,1)}), bf16[128,1,64,256]{3,2,1,0:T(8,128)(2,1)}, u32[]{:S(2)}, u32[]{:S(2)}) async-start(bf16[128,1,64,256]{3,2,1,0:T(8,128)(2,1)} %bitcast.301), calls=%async_computation.2 | async-start | bytes 8388608 | tf_op jit(solution)/shard_map/all_to_all | solution.py:90
  65.6 3.5 collective-permute-start
  69.2 2.1 collective-permute-start.1
  72.0 72.9 %collective-permute-done = bf16[64,256]{1,0:T(8,128)(2,1)S(1)} collective-permute-done((bf16[64,256]{1,0:T(8,128)(2,1)S(1)}, bf16[64,256]{1,0:T(8,128)(2,1)S(1)}, u32[]{:S(2)}, u32[]{:S(2)}) %collective-permute-start) | collective-permute-done | bytes 32800 | tf_op jit(solution)/shard_map/ppermute | solution.py:22
  144.8 7.2 %collective-permute-done.1 = bf16[64,256]{1,0:T(8,128)(2,1)S(1)} collective-permute-done((bf16[64,256]{1,0:T(8,128)(2,1)S(1)}, bf16[64,256]{1,0:T(8,128)(2,1)S(1)}, u32[]{:S(2)}, u32[]{:S(2)}) %collective-permute-start.1) | collective-permute-done | bytes 32800 | tf_op jit(solution)/shard_map/ppermute | solution.py:24
  152.1 164.7 %all-reduce.10.cloned.1.call-done = (bf16[1,64,256]{2,1,0:T(8,128)(2,1)}, bf16[1,64,256]{2,1,0:T(8,128)(2,1)}) async-done(((bf16[1,64,256]{2,1,0:T(8,128)(2,1)}, bf16[1,64,256]{2,1,0:T(8,128)(2,1)}), (bf16[1,64,256]{2,1,0:T(8,128)(2,1)}, bf16[1,64,256]{2,1,0:T(8,128)(2,1)})) %all-reduce.10.cloned.1.call-update) | async-done | bytes 65552 | tf_op jit(solution)/shard_map/psum | solution.py:33
  316.8 3.9 pad_maximum_fusion.1
  320.6 18.4 %while.24 = (s32[]{:T(128)}, bf16[4,64,8,128]{3,1,2,0:T(8,128)(2,1)S(1)}, f32[4,8,64,1]{2,1,3,0:T(8,128)S(1)}, s32[4,13]{1,0:T(4,128)S(1)}, bf16[136,64,256]{2,1...) while((s32[]{:T(128)}, ...), condition=%wide.region_7.8_spmd, body=%wide.region_4.7_spmd.sunk | while | flops 221151776 | bytes 6817576 | solution.py:124
  320.8 2.8 gather_fusion
  325.4 2.8 gather_fusion
  330.0 2.8 gather_fusion
  334.6 2.8 gather_fusion
  339.0 29.0 %while.25 = (s32[]{:T(128)}, bf16[4,64,8,128]{3,2,1,0:T(8,128)(2,1)}, f32[4,13,64,256]{3,2,1,0:T(8,128)}, s32[4,13]{1,0:T(4,128)S(1)}, bf16[136,64,256]{2,1,0:T(...) while((s32[]{:T(128)}, ...), condition=%wide.region_10.11_spmd, body=%wide.region_8.10_spmd.sunk | while | flops 548954624 | bytes 15144784 | solution.py:156
  339.4 2.8 gather_fusion.1
  345.3 1.0 constant_dynamic-update-slice_fusion.2
  346.7 2.8 gather_fusion.1
  352.6 1.0 constant_dynamic-update-slice_fusion.2
  354.0 2.8 gather_fusion.1
  359.9 1.0 constant_dynamic-update-slice_fusion.2
  361.2 2.8 gather_fusion.1
  367.1 1.0 constant_dynamic-update-slice_fusion.2
  368.0 2.4 convert.16
  371.2 1.4 convolution_convert_fusion.1
  372.5 3.2 copy.125
  375.8 6.8 %all-to-all-start.3 = ((bf16[128,1,64,256]{3,2,1,0:T(8,128)(2,1)}), bf16[128,1,64,256]{3,2,1,0:T(8,128)(2,1)}, u32[]{:S(2)}, u32[]{:S(2)}) async-start(bf16[128,1,64,256]{3,2,1,0:T(8,128)(2,1)} %bitcast.302), calls=%async_computation.3 | async-start | bytes 8388608 | tf_op jit(solution)/shard_map/all_to_all | solution.py:193
  382.7 4.0 copy.97
  387.4 0.8 slice_bitcast_fusion.16
  388.2 3.2 collective-permute-start.2
  391.4 2.1 collective-permute-start.3
  393.6 1.1 slice_bitcast_fusion.11
  394.7 74.3 %collective-permute-done.2 = bf16[64,256]{1,0:T(8,128)(2,1)S(1)} collective-permute-done((bf16[64,256]{1,0:T(8,128)(2,1)S(1)}, bf16[64,256]{1,0:T(8,128)(2,1)S(1)}, u32[]{:S(2)}, u32[]{:S(2)}) %collective-permute-start.2) | collective-permute-done | bytes 32800 | tf_op jit(solution)/shard_map/ppermute | solution.py:22
  469.0 6.2 collective-permute-done.3
  475.3 166.2 %all-reduce.8.cloned.1.call-done = f32[2,64,256]{2,1,0:T(8,128)} async-done(((f32[2,64,256]{2,1,0:T(8,128)}), f32[2,64,256]{2,1,0:T(8,128)}) %all-reduce.8.cloned.1.call-update) | async-done | bytes 131088 | tf_op jit(solution)/shard_map/psum | solution.py:182
  641.5 1.0 select_reduce_fusion
  642.5 6.9 %copy.109 = bf16[128,1,64,256]{0,3,2,1:T(8,128)(2,1)} copy(bf16[128,1,64,256]{3,2,1,0:T(8,128)(2,1)} %all-to-all-done.3) | data formatting | bytes 8388608 | tf_op jit(solution)/shard_map/reshape | solution.py:203
  649.5 3.5 fusion.35
  654.9 4.0 all-to-all-start.4
  659.2 0.9 copy.139
  660.1 0.9 copy.140
  661.0 3.5 all-to-all-done.4
  (171 shorter events, 29.4 us)
Async XLA Ops:
  7.2 20.3 %copy-start = (bf16[64,512]{1,0:T(8,128)(2,1)S(1)}, bf16[64,512]{1,0:T(8,128)(2,1)}, u32[]{:S(2)}) copy-start(bf16[64,512]{1,0:T(8,128)(2,1)} %param.11) | copy-start | bytes 196612
  9.0 29.8 %all-to-all-start.1 = ((s32[128,1,1]{2,1,0:T(1,128)}), s32[128,1,1]{2,1,0:T(1,128)S(1)}, u32[]{:S(2)}, u32[]{:S(2)}) async-start(s32[128,1,1]{2,1,0:T(1,128)} %copy.90), calls=%async_computation.1 | async-start | bytes 131072 | tf_op jit(solution)/shard_map/all_to_all | solution.py:86
  38.9 8.8 %all-to-all-start = ((bf16[64,4,256]{2,0,1:T(8,128)(2,1)}), bf16[64,4,256]{2,0,1:T(8,128)(2,1)S(1)}, u32[]{:S(2)}, u32[]{:S(2)}) async-start(bf16[64,4,256]{2,0,1:T(8,128)(2,1)} %pad_maximum_fusion.3), calls=%async_computation | async-start | bytes 262144 | tf_op jit(solution)/shard_map/all_to_all | solution.py:59
  50.5 8.5 %copy-start.9 = (s32[2]{0:T(128)S(1)}, s32[2]{0:T(128)}, u32[]{:S(2)}) copy-start(s32[2]{0:T(128)} %param.15) | copy-start | bytes 28
  50.5 14.6 %copy-start.5 = (bf16[256,1024]{1,0:T(8,128)(2,1)S(1)}, bf16[256,1024]{1,0:T(8,128)(2,1)}, u32[]{:S(2)}) copy-start(bf16[256,1024]{1,0:T(8,128)(2,1)} %param.10) | copy-start | bytes 1572868
  50.5 14.8 %copy-start.6 = (bf16[256,1024]{1,0:T(8,128)(2,1)S(1)}, bf16[256,1024]{1,0:T(8,128)(2,1)}, u32[]{:S(2)}) copy-start(bf16[256,1024]{1,0:T(8,128)(2,1)} %param.13) | copy-start | bytes 1572868
  50.5 14.9 %copy-start.8 = (s32[4,8]{1,0:T(4,128)S(1)}, s32[4,8]{1,0:T(4,128)}, u32[]{:S(2)}) copy-start(s32[4,8]{1,0:T(4,128)} %param.14) | copy-start | bytes 388
  50.5 266.3 %all-to-all-start.2 = ((bf16[128,1,64,256]{3,2,1,0:T(8,128)(2,1)}), bf16[128,1,64,256]{3,2,1,0:T(8,128)(2,1)}, u32[]{:S(2)}, u32[]{:S(2)}) async-start(bf16[128,1,64,256]{3,2,1,0:T(8,128)(2,1)} %bitcast.301), calls=%async_computation.2 | async-start | bytes 8388608 | tf_op jit(solution)/shard_map/all_to_all | solution.py:90
  58.9 257.8 %all-reduce.10.cloned.1.call-start = ((), (), s32[]{:S(2)}) async-start(), calls=%async_computation.6 | async-start | bytes 131072 | tf_op jit(solution)/shard_map/psum | solution.py:33
  65.6 79.2 %collective-permute-start = (bf16[64,256]{1,0:T(8,128)(2,1)S(1)}, bf16[64,256]{1,0:T(8,128)(2,1)S(1)}, u32[]{:S(2)}, u32[]{:S(2)}) collective-permute-start(bf16[64,256]{1,0:T(8,128)(2,1)S(1)} %get-tuple-element.230), channel_id=1, source_target_pairs={{0,4},{4,8},{8,12},{12,16},{16,20},{20,24},{24,28},{28,32},{32,36}... | collective-permute-start | bytes 98312 | tf_op jit(solution)/shard_map/ppermute | solution.py:22
  69.2 82.9 %collective-permute-start.1 = (bf16[64,256]{1,0:T(8,128)(2,1)S(1)}, bf16[64,256]{1,0:T(8,128)(2,1)S(1)}, u32[]{:S(2)}, u32[]{:S(2)}) collective-permute-start(bf16[64,256]{1,0:T(8,128)(2,1)S(1)} %get-tuple-element.231), channel_id=1, source_target_pairs={{4,0},{8,4},{12,8},{16,12},{20,16},{24,20},{28,24},{32,28},{36,32}... | collective-permute-start | bytes 98312 | tf_op jit(solution)/shard_map/ppermute | solution.py:24
  368.0 2.5 copy-start.3
  370.4 2.1 copy-start.2
  375.8 6.9 %copy-start.1 = (f32[4,13,64,256]{3,2,1,0:T(8,128)S(1)}, f32[4,13,64,256]{3,2,1,0:T(8,128)}, u32[]{:S(2)}) copy-start(f32[4,13,64,256]{3,2,1,0:T(8,128)} %get-tuple-element.98) | copy-start | bytes 10223620
  375.8 266.8 %all-to-all-start.3 = ((bf16[128,1,64,256]{3,2,1,0:T(8,128)(2,1)}), bf16[128,1,64,256]{3,2,1,0:T(8,128)(2,1)}, u32[]{:S(2)}, u32[]{:S(2)}) async-start(bf16[128,1,64,256]{3,2,1,0:T(8,128)(2,1)} %bitcast.302), calls=%async_computation.3 | async-start | bytes 8388608 | tf_op jit(solution)/shard_map/all_to_all | solution.py:193
  382.5 258.9 %all-reduce.8.cloned.1.call-start = ((), (), s32[]{:S(2)}) async-start(), calls=%async_computation.5 | async-start | bytes 262144 | tf_op jit(solution)/shard_map/psum | solution.py:182
  388.2 80.8 %collective-permute-start.2 = (bf16[64,256]{1,0:T(8,128)(2,1)S(1)}, bf16[64,256]{1,0:T(8,128)(2,1)S(1)}, u32[]{:S(2)}, u32[]{:S(2)}) collective-permute-start(bf16[64,256]{1,0:T(8,128)(2,1)S(1)} %get-tuple-element.226), channel_id=1, source_target_pairs={{0,4},{4,8},{8,12},{12,16},{16,20},{20,24},{24,28},{28,32},{32,36}... | collective-permute-start | bytes 98312 | tf_op jit(solution)/shard_map/ppermute | solution.py:22
  391.4 83.8 %collective-permute-start.3 = (bf16[64,256]{1,0:T(8,128)(2,1)S(1)}, bf16[64,256]{1,0:T(8,128)(2,1)S(1)}, u32[]{:S(2)}, u32[]{:S(2)}) collective-permute-start(bf16[64,256]{1,0:T(8,128)(2,1)S(1)} %get-tuple-element.227), channel_id=1, source_target_pairs={{4,0},{8,4},{12,8},{16,12},{20,16},{24,20},{28,24},{32,28},{36,32}... | collective-permute-start | bytes 98312 | tf_op jit(solution)/shard_map/ppermute | solution.py:24
  649.4 9.4 %copy-start.4 = (bf16[4,64,8,128]{3,1,2,0:T(8,128)(2,1)S(1)}, bf16[4,64,8,128]{3,1,2,0:T(8,128)(2,1)}, u32[]{:S(2)}) copy-start(bf16[4,64,8,128]{3,1,2,0:T(8,128)(2,1)} %copy-done.3) | copy-start | bytes 1572868
  649.5 9.7 %copy-start.7 = (bf16[4,64,8,128]{3,2,1,0:T(8,128)(2,1)S(1)}, bf16[4,64,8,128]{3,2,1,0:T(8,128)(2,1)}, u32[]{:S(2)}) copy-start(bf16[4,64,8,128]{3,2,1,0:T(8,128)(2,1)} %get-tuple-element.97) | copy-start | bytes 1572868
  654.9 9.6 %all-to-all-start.4 = ((bf16[4,2,8192]{2,1,0:T(2,128)(2,1)}), bf16[4,2,8192]{2,1,0:T(2,128)(2,1)S(1)}, u32[]{:S(2)}, u32[]{:S(2)}) async-start(bf16[4,2,8192]{2,1,0:T(2,128)(2,1)} %reshape.443), calls=%async_computation.4 | async-start | bytes 262144 | tf_op jit(solution)/shard_map/all_to_all | solution.py:207
Sparse Core Ops, SparseCore 0:
  72.1 244.6 all-reduce.9
  387.5 253.9 all-reduce.7
where the time goes:
time: 674 us; the launch traced here: 673 us
  waiting for transfers between devices  507 us (75%)
  local copies, waits for them, and re-layouts  59.1 us (9%)
  starting transfers between devices  52.7 us (8%)
  between operations  19.6 us (3%)
  matrix products  17.9 us (3%)
  other arithmetic  15.6 us (2%)
    psum x1, waiting for transfers between devices, body(): global_total = lax.psum(global_terms, 'seq')  166 us
    psum x1, waiting for transfers between devices, broadcast(): return lax.psum(block, axis)  165 us
    ppermute x2, waiting for transfers between devices, padded_2(): lax.ppermute(tail, axis, [(i, (i + 1) % count) for i in range(ends)])  147 us
    gather x8, local copies, waits for them, and re-layouts, key_rows(): chosen = library[spots]  22.7 us
    all_to_all x1, starting transfers between devices, body(): lax.all_to_all(wanted, 'seq', split_axis=0, concat_axis=0, tiled=True)  18.4 us
  transfers between devices with their start and end apart: 11, of which 9 were waited for; matrix products, arithmetic and copies ran while one was open for 2% of the time, Pallas kernels for 0%

commit v1 on v0

--- a/solution.py
+++ b/solution.py
@@ -179,7 +179,7 @@
     )
     grads = grads + edge_first + edge_last
     global_terms = jnp.sum(terms[:, 3 : 3 + GLOB], axis=0)
-    global_total = lax.psum(global_terms, "seq")
+    global_total = jnp.sum(lax.all_gather(global_terms, "seq"), axis=0)
     global_hits = ((glob_blocks // blocks_here)[:, None] == here) & (
         (glob_blocks % blocks_here)[:, None] == block_ids[None, :]
     )

time: 674 us -> 580 us (0.86)
  waiting for transfers between devices: 507 us -> 409 us
  other arithmetic: 15.6 us -> 22.5 us
    psum x1 -> x0, waiting for transfers between devices: 166 us -> none  [body(): global_total = lax.psum(global_terms, 'seq')]
    all_gather x0 -> x1, waiting for transfers between devices: none -> 57.6 us  [body(): global_total = jnp.sum(lax.all_gather(global_terms, 'seq'), axis=0)]
    ppermute x2, waiting for transfers between devices: 147 us -> 155 us  [padded_2(): lax.ppermute(tail, axis, [(i, (i + 1) % count) for i in range(ends)])]
    reduce_sum x0 -> x1, other arithmetic: none -> 6.82 us  [body(): global_total = jnp.sum(lax.all_gather(global_terms, 'seq'), axis=0)]
  transfers between devices with their start and end apart: 11 -> 11, of which waited for: 9 -> 10; matrix products, arithmetic and copies ran while one was open for 2% -> 4% of each run, Pallas kernels for 0% -> 0%
where the time goes in v1:
time: 580 us; the launch traced here: 578 us
  waiting for transfers between devices  409 us (71%)
  local copies, waits for them, and re-layouts  56.4 us (10%)
  starting transfers between devices  52.7 us (9%)
  other arithmetic  22.5 us (4%)
  between operations  19.6 us (3%)
  matrix products  17.9 us (3%)
    psum x1, waiting for transfers between devices, broadcast(): return lax.psum(block, axis)  165 us
    ppermute x2, waiting for transfers between devices, padded_2(): lax.ppermute(tail, axis, [(i, (i + 1) % count) for i in range(ends)])  155 us
    all_gather x1, waiting for transfers between devices, body(): global_total = jnp.sum(lax.all_gather(global_terms, 'seq'), axis=0)  57.6 us
    gather x8, local copies, waits for them, and re-layouts, key_rows(): chosen = library[spots]  22.7 us
    all_to_all x1, starting transfers between devices, body(): lax.all_to_all(wanted, 'seq', split_axis=0, concat_axis=0, tiled=True)  18.4 us
    ppermute x2, waiting for transfers between devices, padded_2(): lax.ppermute(head, axis, [((i + 1) % count, i) for i in range(ends)])  11.8 us
  transfers between devices with their start and end apart: 11, of which 10 were waited for; matrix products, arithmetic and copies ran while one was open for 4% of the time, Pallas kernels for 0%

profile of v1, /device:TPU:1, one launch (start us, length us, event | category | flops | bytes accessed | tf_op | source)
XLA Modules:
  0.0 578.3 jit_solution(6696569952455034976)
XLA Ops:
  9.0 18.4 %all-to-all-start.1 = ((s32[128,1,1]{2,1,0:T(1,128)}), s32[128,1,1]{2,1,0:T(1,128)S(1)}, u32[]{:S(2)}, u32[]{:S(2)}) async-start(s32[128,1,1]{2,1,0:T(1,128)} %copy.90), calls=%async_computation.1 | async-start | bytes 131072 | tf_op jit(solution)/shard_map/all_to_all | solution.py:86
  27.5 0.9 copy_bitcast_fusion.7
  29.0 9.9 %all-to-all-done.1 = s32[128,1,1]{2,1,0:T(1,128)S(1)} async-done(((s32[128,1,1]{2,1,0:T(1,128)}), s32[128,1,1]{2,1,0:T(1,128)S(1)}, u32[]{:S(2)}, u32[]{:S(2)}) %all-to-all-start.1) | async-done | bytes 544 | tf_op jit(solution)/shard_map/all_to_all | solution.py:86
  38.9 4.0 all-to-all-start
  42.9 2.3 reduce
  45.2 2.5 all-to-all-done
  47.7 2.8 gather_fusion.2
  50.5 8.4 %all-to-all-start.2 = ((bf16[128,1,64,256]{3,2,1,0:T(8,128)(2,1)}), bf16[128,1,64,256]{3,2,1,0:T(8,128)(2,1)}, u32[]{:S(2)}, u32[]{:S(2)}) async-start(bf16[128,1,64,256]{3,2,1,0:T(8,128)(2,1)} %bitcast.303), calls=%async_computation.2 | async-start | bytes 8388608 | tf_op jit(solution)/shard_map/all_to_all | solution.py:90
  65.7 3.5 collective-permute-start
  69.2 1.9 collective-permute-start.1
  72.0 72.8 %collective-permute-done = bf16[64,256]{1,0:T(8,128)(2,1)S(1)} collective-permute-done((bf16[64,256]{1,0:T(8,128)(2,1)S(1)}, bf16[64,256]{1,0:T(8,128)(2,1)S(1)}, u32[]{:S(2)}, u32[]{:S(2)}) %collective-permute-start) | collective-permute-done | bytes 32800 | tf_op jit(solution)/shard_map/ppermute | solution.py:22
  144.9 7.2 %collective-permute-done.1 = bf16[64,256]{1,0:T(8,128)(2,1)S(1)} collective-permute-done((bf16[64,256]{1,0:T(8,128)(2,1)S(1)}, bf16[64,256]{1,0:T(8,128)(2,1)S(1)}, u32[]{:S(2)}, u32[]{:S(2)}) %collective-permute-start.1) | collective-permute-done | bytes 32800 | tf_op jit(solution)/shard_map/ppermute | solution.py:24
  152.1 165.0 %all-reduce.7.cloned.1.call-done = (bf16[1,64,256]{2,1,0:T(8,128)(2,1)}, bf16[1,64,256]{2,1,0:T(8,128)(2,1)}) async-done(((bf16[1,64,256]{2,1,0:T(8,128)(2,1)}, bf16[1,64,256]{2,1,0:T(8,128)(2,1)}), (bf16[1,64,256]{2,1,0:T(8,128)(2,1)}, bf16[1,64,256]{2,1,0:T(8,128)(2,1)})) %all-reduce.7.cloned.1.call-update) | async-done | bytes 65552 | tf_op jit(solution)/shard_map/psum | solution.py:33
  317.1 3.9 pad_maximum_fusion.1
  321.0 18.4 %while.24 = (s32[]{:T(128)}, bf16[4,64,8,128]{3,1,2,0:T(8,128)(2,1)S(1)}, f32[4,8,64,1]{2,1,3,0:T(8,128)S(1)}, s32[4,13]{1,0:T(4,128)S(1)}, bf16[136,64,256]{2,1...) while((s32[]{:T(128)}, ...), condition=%wide.region_7.8_spmd, body=%wide.region_4.7_spmd.sunk | while | flops 221151776 | bytes 6817576 | solution.py:124
  321.2 2.8 gather_fusion
  325.8 2.8 gather_fusion
  330.4 2.8 gather_fusion
  335.0 2.8 gather_fusion
  339.4 29.0 %while.25 = (s32[]{:T(128)}, bf16[4,64,8,128]{3,2,1,0:T(8,128)(2,1)}, f32[4,13,64,256]{3,2,1,0:T(8,128)}, s32[4,13]{1,0:T(4,128)S(1)}, bf16[136,64,256]{2,1,0:T(...) while((s32[]{:T(128)}, ...), condition=%wide.region_10.11_spmd, body=%wide.region_8.10_spmd.sunk | while | flops 548954624 | bytes 15144784 | solution.py:156
  339.8 2.8 gather_fusion.1
  345.7 1.0 constant_dynamic-update-slice_fusion.2
  347.1 2.8 gather_fusion.1
  353.0 1.0 constant_dynamic-update-slice_fusion.2
  354.3 2.8 gather_fusion.1
  360.2 1.0 constant_dynamic-update-slice_fusion.2
  361.5 2.8 gather_fusion.1
  367.4 0.9 constant_dynamic-update-slice_fusion.2
  368.4 1.9 slice_reduce_fusion
  370.3 2.2 convert.16
  373.2 1.4 convolution_convert_fusion.1
  374.6 3.2 copy.125
  377.8 6.8 %all-to-all-start.3 = ((bf16[128,1,64,256]{3,2,1,0:T(8,128)(2,1)}), bf16[128,1,64,256]{3,2,1,0:T(8,128)(2,1)}, u32[]{:S(2)}, u32[]{:S(2)}) async-start(bf16[128,1,64,256]{3,2,1,0:T(8,128)(2,1)} %bitcast.304), calls=%async_computation.3 | async-start | bytes 8388608 | tf_op jit(solution)/shard_map/all_to_all | solution.py:193
  384.7 2.2 copy.97
  387.0 0.9 slice_bitcast_fusion.16
  387.8 3.2 collective-permute-start.2
  391.0 2.1 collective-permute-start.3
  393.3 82.1 %collective-permute-done.2 = bf16[64,256]{1,0:T(8,128)(2,1)S(1)} collective-permute-done((bf16[64,256]{1,0:T(8,128)(2,1)S(1)}, bf16[64,256]{1,0:T(8,128)(2,1)S(1)}, u32[]{:S(2)}, u32[]{:S(2)}) %collective-permute-start.2) | collective-permute-done | bytes 32800 | tf_op jit(solution)/shard_map/ppermute | solution.py:22
  475.5 4.6 collective-permute-done.3
  480.2 4.1 all-to-all-done.3
  484.4 6.9 %copy.109 = bf16[128,1,64,256]{0,3,2,1:T(8,128)(2,1)} copy(bf16[128,1,64,256]{3,2,1,0:T(8,128)(2,1)} %all-to-all-done.3) | data formatting | bytes 8388608 | tf_op jit(solution)/shard_map/reshape | solution.py:203
  491.3 57.6 %all-gather.3.cloned.1.call-done = f32[256,64,256]{2,1,0:T(8,128)} async-done(((f32[2,64,256]{2,1,0:T(8,128)}), f32[256,64,256]{2,1,0:T(8,128)}) %all-gather.3.cloned.1.call-update) | async-done | bytes 16777232 | tf_op jit(solution)/shard_map/all_gather | solution.py:182
  548.9 6.8 %reduce_sum.69 = f32[2,64,256]{2,1,0:T(8,128)S(1)} reduce(f32[128,2,64,256]{3,2,1,0:T(8,128)} %bitcast.302, f32[]{:T(128)} %constant.151.clone.1), dimensions={0}, to_apply=%region_12.13 | reduce | flops 4161536 | bytes 16908292 | tf_op jit(solution)/shard_map/reduce_sum | solution.py:182
  555.8 3.5 fusion.35
  561.2 4.0 all-to-all-start.4
  565.6 0.9 copy.139
  566.4 0.9 copy.140
  567.3 2.7 all-to-all-done.4
  (176 shorter events, 29.9 us)
Async XLA Ops:
  7.2 20.3 %copy-start = (bf16[64,512]{1,0:T(8,128)(2,1)S(1)}, bf16[64,512]{1,0:T(8,128)(2,1)}, u32[]{:S(2)}) copy-start(bf16[64,512]{1,0:T(8,128)(2,1)} %param.11) | copy-start | bytes 196612
  9.0 29.8 %all-to-all-start.1 = ((s32[128,1,1]{2,1,0:T(1,128)}), s32[128,1,1]{2,1,0:T(1,128)S(1)}, u32[]{:S(2)}, u32[]{:S(2)}) async-start(s32[128,1,1]{2,1,0:T(1,128)} %copy.90), calls=%async_computation.1 | async-start | bytes 131072 | tf_op jit(solution)/shard_map/all_to_all | solution.py:86
  38.9 8.8 %all-to-all-start = ((bf16[64,4,256]{2,0,1:T(8,128)(2,1)}), bf16[64,4,256]{2,0,1:T(8,128)(2,1)S(1)}, u32[]{:S(2)}, u32[]{:S(2)}) async-start(bf16[64,4,256]{2,0,1:T(8,128)(2,1)} %pad_maximum_fusion.3), calls=%async_computation | async-start | bytes 262144 | tf_op jit(solution)/shard_map/all_to_all | solution.py:59
  50.5 8.5 %copy-start.11 = (s32[2]{0:T(128)S(1)}, s32[2]{0:T(128)}, u32[]{:S(2)}) copy-start(s32[2]{0:T(128)} %param.15) | copy-start | bytes 28
  50.5 14.6 %copy-start.7 = (bf16[256,1024]{1,0:T(8,128)(2,1)S(1)}, bf16[256,1024]{1,0:T(8,128)(2,1)}, u32[]{:S(2)}) copy-start(bf16[256,1024]{1,0:T(8,128)(2,1)} %param.10) | copy-start | bytes 1572868
  50.5 14.8 %copy-start.8 = (bf16[256,1024]{1,0:T(8,128)(2,1)S(1)}, bf16[256,1024]{1,0:T(8,128)(2,1)}, u32[]{:S(2)}) copy-start(bf16[256,1024]{1,0:T(8,128)(2,1)} %param.13) | copy-start | bytes 1572868
  50.5 14.9 %copy-start.10 = (s32[4,8]{1,0:T(4,128)S(1)}, s32[4,8]{1,0:T(4,128)}, u32[]{:S(2)}) copy-start(s32[4,8]{1,0:T(4,128)} %param.14) | copy-start | bytes 388
  50.5 266.6 %all-to-all-start.2 = ((bf16[128,1,64,256]{3,2,1,0:T(8,128)(2,1)}), bf16[128,1,64,256]{3,2,1,0:T(8,128)(2,1)}, u32[]{:S(2)}, u32[]{:S(2)}) async-start(bf16[128,1,64,256]{3,2,1,0:T(8,128)(2,1)} %bitcast.303), calls=%async_computation.2 | async-start | bytes 8388608 | tf_op jit(solution)/shard_map/all_to_all | solution.py:90
  58.9 258.2 %all-reduce.7.cloned.1.call-start = ((), (), s32[]{:S(2)}) async-start(), calls=%async_computation.6 | async-start | bytes 131072 | tf_op jit(solution)/shard_map/psum | solution.py:33
  65.7 79.2 %collective-permute-start = (bf16[64,256]{1,0:T(8,128)(2,1)S(1)}, bf16[64,256]{1,0:T(8,128)(2,1)S(1)}, u32[]{:S(2)}, u32[]{:S(2)}) collective-permute-start(bf16[64,256]{1,0:T(8,128)(2,1)S(1)} %get-tuple-element.230), channel_id=1, source_target_pairs={{0,4},{4,8},{8,12},{12,16},{16,20},{20,24},{24,28},{28,32},{32,36}... | collective-permute-start | bytes 98312 | tf_op jit(solution)/shard_map/ppermute | solution.py:22
  69.2 82.9 %collective-permute-start.1 = (bf16[64,256]{1,0:T(8,128)(2,1)S(1)}, bf16[64,256]{1,0:T(8,128)(2,1)S(1)}, u32[]{:S(2)}, u32[]{:S(2)}) collective-permute-start(bf16[64,256]{1,0:T(8,128)(2,1)S(1)} %get-tuple-element.231), channel_id=1, source_target_pairs={{4,0},{8,4},{12,8},{16,12},{20,16},{24,20},{28,24},{32,28},{36,32}... | collective-permute-start | bytes 98312 | tf_op jit(solution)/shard_map/ppermute | solution.py:24
  71.8 477.1 %all-gather.3.cloned.1.call-start = ((), (), s32[]{:S(2)}) async-start(), calls=%async_computation.5 | async-start | bytes 16908288 | tf_op jit(solution)/shard_map/all_gather | solution.py:182
  368.4 4.3 copy-start.5
  372.5 2.1 copy-start.4
  377.8 6.9 %copy-start.2 = (f32[4,13,64,256]{3,2,1,0:T(8,128)S(1)}, f32[4,13,64,256]{3,2,1,0:T(8,128)}, u32[]{:S(2)}) copy-start(f32[4,13,64,256]{3,2,1,0:T(8,128)} %get-tuple-element.98) | copy-start | bytes 10223620
  377.8 106.5 %all-to-all-start.3 = ((bf16[128,1,64,256]{3,2,1,0:T(8,128)(2,1)}), bf16[128,1,64,256]{3,2,1,0:T(8,128)(2,1)}, u32[]{:S(2)}, u32[]{:S(2)}) async-start(bf16[128,1,64,256]{3,2,1,0:T(8,128)(2,1)} %bitcast.304), calls=%async_computation.3 | async-start | bytes 8388608 | tf_op jit(solution)/shard_map/all_to_all | solution.py:193
  387.0 6.2 %copy-start.3 = (f32[4,13,64,256]{3,0,2,1:T(4,128)}, f32[4,13,64,256]{3,0,2,1:T(4,128)S(1)}, u32[]{:S(2)}) copy-start(f32[4,13,64,256]{3,0,2,1:T(4,128)S(1)} %copy.97) | copy-start | bytes 10223620
  387.8 87.6 %collective-permute-start.2 = (bf16[64,256]{1,0:T(8,128)(2,1)S(1)}, bf16[64,256]{1,0:T(8,128)(2,1)S(1)}, u32[]{:S(2)}, u32[]{:S(2)}) collective-permute-start(bf16[64,256]{1,0:T(8,128)(2,1)S(1)} %get-tuple-element.226), channel_id=1, source_target_pairs={{0,4},{4,8},{8,12},{12,16},{16,20},{20,24},{24,28},{28,32},{32,36}... | collective-permute-start | bytes 98312 | tf_op jit(solution)/shard_map/ppermute | solution.py:22
  391.0 89.1 %collective-permute-start.3 = (bf16[64,256]{1,0:T(8,128)(2,1)S(1)}, bf16[64,256]{1,0:T(8,128)(2,1)S(1)}, u32[]{:S(2)}, u32[]{:S(2)}) collective-permute-start(bf16[64,256]{1,0:T(8,128)(2,1)S(1)} %get-tuple-element.227), channel_id=1, source_target_pairs={{4,0},{8,4},{12,8},{16,12},{20,16},{24,20},{28,24},{32,28},{36,32}... | collective-permute-start | bytes 98312 | tf_op jit(solution)/shard_map/ppermute | solution.py:24
  555.7 9.5 %copy-start.6 = (bf16[4,64,8,128]{3,1,2,0:T(8,128)(2,1)S(1)}, bf16[4,64,8,128]{3,1,2,0:T(8,128)(2,1)}, u32[]{:S(2)}) copy-start(bf16[4,64,8,128]{3,1,2,0:T(8,128)(2,1)} %copy-done.5) | copy-start | bytes 1572868
  555.8 9.8 %copy-start.9 = (bf16[4,64,8,128]{3,2,1,0:T(8,128)(2,1)S(1)}, bf16[4,64,8,128]{3,2,1,0:T(8,128)(2,1)}, u32[]{:S(2)}) copy-start(bf16[4,64,8,128]{3,2,1,0:T(8,128)(2,1)} %get-tuple-element.97) | copy-start | bytes 1572868
  555.8 15.7 %copy-start.1 = (bf16[64,512]{1,0:T(8,128)(2,1)S(1)}, bf16[64,512]{1,0:T(8,128)(2,1)}, u32[]{:S(2)}) copy-start(bf16[64,512]{1,0:T(8,128)(2,1)} %param.11) | copy-start | bytes 196612
  561.2 8.8 %all-to-all-start.4 = ((bf16[4,2,8192]{2,1,0:T(2,128)(2,1)}), bf16[4,2,8192]{2,1,0:T(2,128)(2,1)S(1)}, u32[]{:S(2)}, u32[]{:S(2)}) async-start(bf16[4,2,8192]{2,1,0:T(2,128)(2,1)} %reshape.444), calls=%async_computation.4 | async-start | bytes 262144 | tf_op jit(solution)/shard_map/all_to_all | solution.py:207
Sparse Core Ops, SparseCore 0:
  71.9 245.1 all-reduce.6
  370.4 178.3 all-gather.2
